TPU v7x, 256 devices: a whole 4x4x8 slice. The times are simulated.
256 devices in a mesh: seq: 64 (over y, z, core), head: 4 (over x).
Axes of the slice: x: 4, y: 4, z: 8, core: 2. Of those that a mesh axis runs over, the one named last changes fastest.
Arguments:
- queries: bfloat16 [65536, 512], P('seq', 'head'), may hold values from -6 to 6
- keys: bfloat16 [65536, 512], P('seq', 'head'), may hold values from -6 to 6
- values: bfloat16 [65536, 512], P('seq', 'head'), may hold values from -6 to 6
- outputs: bfloat16 [65536, 512], P('seq', 'head'), may hold values from -6 to 6
- d_outputs: bfloat16 [65536, 512], P('seq', 'head'), may hold values from -6 to 6
- log_norm: float32 [8, 65536], P('head', 'seq'), may hold values from 4 to 5.5
- rand_owner: int32 [512, 3], P('seq'), may hold values from 0 to 63, all different within a row; in each aligned block of 8 rows (0 to 7, 8 to 15, ...) at most 2 rows name the same one
- rand_local: int32 [512, 3], P('seq'), may hold values from 0 to 7
- glob_blocks: int32 [2], replicated, may hold values from 0 to 511
Outputs:
- d_queries: bfloat16 [65536, 512], P('seq', 'head')
- d_keys: bfloat16 [65536, 512], P('seq', 'head')
- d_values: bfloat16 [65536, 512], P('seq', 'head')
Inputs may be any that keep to these rules, and one draw needn't show every extreme that they name: `rand_owner`: each row names 3 different seq indices; within the 8 rows of one seq index no value is named more than 2 times, a bound that some block reaches.
All inputs are finite; a program needn't handle non-finite values.
Results may differ from a plain program's by a relative error of at most 0.0085.
Values may be sent and summed in bfloat16 or wider, within the bound.
A program may use at most 128 MiB of HBM per device.

v0:
```python
import math
import jax
import jax.numpy as jnp
from jax import lax
from jax.sharding import PartitionSpec as P

BLOCK = 128


def extended(array, sides, width):
    for axis, dim in sides:
        size, length = (lax.axis_size(axis), array.shape[dim])
        up = [(i, (i + 1) % size) for i in range(size - 1)]
        down = [(j, i) for i, j in up]
        last = lax.slice_in_dim(array, length - width, length, axis=dim)
        leading = lax.slice_in_dim(array, 0, width, axis=dim)
        before = lax.ppermute(last, axis, up)
        after = lax.ppermute(leading, axis, down)
        array = jnp.concatenate([before, array, after], axis=dim)
    return array


def pair_terms(query_rows, grad_rows, norm_rows, delta_rows, key_rows, value_rows, factor):
    scores = (
        jnp.einsum("nqhd,nkhd->nhqk", query_rows, key_rows, preferred_element_type=jnp.float32)
        * factor
    )
    weights = jnp.exp(scores - norm_rows[..., None])
    grad_weights = jnp.einsum(
        "nqhd,nkhd->nhqk", grad_rows, value_rows, preferred_element_type=jnp.float32
    )
    grad_scores = weights * (grad_weights - delta_rows[..., None])
    weights_low = weights.astype(jnp.bfloat16)
    scores_low = grad_scores.astype(jnp.bfloat16)
    grad_query = (
        jnp.einsum("nhqk,nkhd->nqhd", scores_low, key_rows, preferred_element_type=jnp.float32)
        * factor
    )
    grad_key = (
        jnp.einsum("nhqk,nqhd->nkhd", scores_low, query_rows, preferred_element_type=jnp.float32)
        * factor
    )
    grad_value = jnp.einsum(
        "nhqk,nqhd->nkhd", weights_low, grad_rows, preferred_element_type=jnp.float32
    )
    return (grad_query, grad_key, grad_value)


def add_by_block(targets, block_ids, blocks):
    selector = (block_ids[:, None] == jnp.arange(blocks, dtype=jnp.int32)[None, :]).astype(
        jnp.bfloat16
    )
    flat_terms = targets.reshape(targets.shape[0], -1)
    high_part = flat_terms.astype(jnp.bfloat16)
    low_part = (flat_terms - high_part.astype(jnp.float32)).astype(jnp.bfloat16)
    summed = jnp.einsum("sn,sf->nf", selector, high_part, preferred_element_type=jnp.float32)
    summed = summed + jnp.einsum(
        "sn,sf->nf", selector, low_part, preferred_element_type=jnp.float32
    )
    return summed.reshape((blocks,) + targets.shape[1:])


def shards(
    queries, keys, values, outputs, d_outputs, log_norm, rand_owner, rand_local, glob_blocks
):
    tokens_here, features = queries.shape
    heads_here = log_norm.shape[0]
    head_size = features // heads_here
    blocks = tokens_here // BLOCK
    per_block = rand_owner.shape[1]
    factor = 1.0 / math.sqrt(head_size)
    owners = lax.axis_size("seq")
    seq_index = lax.axis_index("seq")
    block_shape = (blocks, BLOCK, heads_here, head_size)
    query_blocks = queries.reshape(block_shape)
    grad_blocks = d_outputs.reshape(block_shape)
    split_out = outputs.reshape(tokens_here, heads_here, head_size).astype(jnp.float32)
    split_grad = d_outputs.reshape(tokens_here, heads_here, head_size).astype(jnp.float32)
    delta_flat = jnp.sum(split_out * split_grad, axis=-1).T
    delta_blocks = delta_flat.reshape(heads_here, blocks, BLOCK).transpose(1, 0, 2)
    norm_blocks = log_norm.reshape(heads_here, blocks, BLOCK).transpose(1, 0, 2)
    d_queries = jnp.zeros(block_shape, jnp.float32)
    pad_shape = (blocks + 2,) + block_shape[1:]
    keys_grad_pad = jnp.zeros(pad_shape, jnp.float32)
    values_grad_pad = jnp.zeros(pad_shape, jnp.float32)
    padded = extended(jnp.stack([keys, values]), (("seq", 1),), BLOCK)
    keys_pad = padded[0].reshape(pad_shape)
    values_pad = padded[1].reshape(pad_shape)
    for offset in range(3):
        grad_query, grad_key, grad_value = pair_terms(
            query_blocks,
            grad_blocks,
            norm_blocks,
            delta_blocks,
            keys_pad[offset : offset + blocks],
            values_pad[offset : offset + blocks],
            factor,
        )
        d_queries = d_queries + grad_query
        keys_grad_pad = keys_grad_pad.at[offset : offset + blocks].add(grad_key)
        values_grad_pad = values_grad_pad.at[offset : offset + blocks].add(grad_value)
    outgoing_edges = jnp.stack(
        [
            jnp.concatenate([keys_grad_pad[0], keys_grad_pad[blocks + 1]], axis=0).reshape(
                2 * BLOCK, features
            ),
            jnp.concatenate([values_grad_pad[0], values_grad_pad[blocks + 1]], axis=0).reshape(
                2 * BLOCK, features
            ),
        ]
    )
    arrived = extended(outgoing_edges.astype(jnp.bfloat16), (("seq", 1),), BLOCK).astype(
        outgoing_edges.dtype
    )
    from_before = arrived[:, :BLOCK].reshape((2,) + block_shape[1:])
    from_after = arrived[:, 3 * BLOCK :].reshape((2,) + block_shape[1:])
    d_keys = (
        keys_grad_pad[1 : blocks + 1].at[0].add(from_before[0]).at[blocks - 1].add(from_after[0])
    )
    d_values = (
        values_grad_pad[1 : blocks + 1].at[0].add(from_before[1]).at[blocks - 1].add(from_after[1])
    )
    global_owner = glob_blocks // blocks
    global_local = glob_blocks % blocks
    owned_here = (global_owner == seq_index).astype(jnp.float32)
    key_table = keys.reshape(blocks, BLOCK, features)
    value_table = values.reshape(blocks, BLOCK, features)
    own_part = jnp.stack([key_table[global_local], value_table[global_local]], axis=1).astype(
        jnp.float32
    )
    own_part = own_part * owned_here[:, None, None, None]
    shared = lax.psum(own_part, "seq").astype(jnp.bfloat16)
    global_pieces = []
    for number in range(shared.shape[0]):
        key_rows = jnp.broadcast_to(shared[number, 0].reshape(block_shape[1:]), block_shape)
        value_rows = jnp.broadcast_to(shared[number, 1].reshape(block_shape[1:]), block_shape)
        grad_query, grad_key, grad_value = pair_terms(
            query_blocks, grad_blocks, norm_blocks, delta_blocks, key_rows, value_rows, factor
        )
        d_queries = d_queries + grad_query
        global_pieces.append(
            jnp.stack(
                [
                    jnp.sum(grad_key, axis=0).reshape(BLOCK, features),
                    jnp.sum(grad_value, axis=0).reshape(BLOCK, features),
                ]
            )
        )
    totals = lax.psum(jnp.stack(global_pieces), "seq")
    for number in range(shared.shape[0]):
        d_keys = d_keys.at[global_local[number]].add(
            owned_here[number] * totals[number, 0].reshape(block_shape[1:])
        )
        d_values = d_values.at[global_local[number]].add(
            owned_here[number] * totals[number, 1].reshape(block_shape[1:])
        )
    references = blocks * per_block
    capacity = max(2, (references + owners - 1) // owners)
    owner_flat = rand_owner.reshape(-1)
    local_flat = rand_local.reshape(-1)
    matches = (owner_flat[:, None] == jnp.arange(owners, dtype=jnp.int32)[None, :]).astype(
        jnp.int32
    )
    within = jnp.sum((jnp.cumsum(matches, axis=0) - 1) * matches, axis=1)
    slot_index = owner_flat * capacity + within
    requested = jnp.zeros((owners * capacity,), jnp.int32).at[slot_index].set(local_flat)
    wanted = lax.all_to_all(
        requested.reshape(owners, capacity), "seq", split_axis=0, concat_axis=0, tiled=True
    )
    wanted_flat = wanted.reshape(-1)
    outgoing = jnp.stack([key_table[wanted_flat], value_table[wanted_flat]], axis=1)
    fetched = lax.all_to_all(
        outgoing.reshape(owners, capacity, 2, BLOCK, features),
        "seq",
        split_axis=0,
        concat_axis=0,
        tiled=True,
    )
    picked = fetched.reshape(owners * capacity, 2, BLOCK, features)[slot_index]
    picked = picked.reshape((blocks, per_block, 2) + block_shape[1:])
    pieces = []
    for column in range(per_block):
        grad_query, grad_key, grad_value = pair_terms(
            query_blocks,
            grad_blocks,
            norm_blocks,
            delta_blocks,
            picked[:, column, 0],
            picked[:, column, 1],
            factor,
        )
        d_queries = d_queries + grad_query
        pieces.append(jnp.stack([grad_key, grad_value], axis=1))
    partials = jnp.stack(pieces, axis=1).reshape(references, 2, BLOCK, features)
    returned = (
        jnp.zeros((owners * capacity, 2, BLOCK, features), jnp.float32).at[slot_index].set(partials)
    )
    received = lax.all_to_all(
        returned.reshape(owners, capacity, 2, BLOCK, features).astype(jnp.bfloat16),
        "seq",
        split_axis=0,
        concat_axis=0,
        tiled=True,
    ).astype(jnp.float32)
    summed = add_by_block(
        received.reshape(owners * capacity, 2, BLOCK, features), wanted_flat, blocks
    )
    d_keys = d_keys + summed[:, 0].reshape(block_shape)
    d_values = d_values + summed[:, 1].reshape(block_shape)
    return (
        d_queries.reshape(tokens_here, features).astype(jnp.bfloat16),
        d_keys.reshape(tokens_here, features).astype(jnp.bfloat16),
        d_values.reshape(tokens_here, features).astype(jnp.bfloat16),
    )


def solution(mesh):
    placed = (
        P("seq", "head"),
        P("seq", "head"),
        P("seq", "head"),
        P("seq", "head"),
        P("seq", "head"),
        P("head", "seq"),
        P("seq", None),
        P("seq", None),
        P(),
    )
    return jax.shard_map(
        shards,
        mesh=mesh,
        in_specs=placed,
        out_specs=(P("seq", "head"), P("seq", "head"), P("seq", "head")),
        check_vma=False,
    )
```

profile of v0, /device:TPU:1, one launch (start us, length us, event | category | flops | bytes accessed | tf_op | source)
XLA Modules:
  0.0 938.5 jit_solution(7537119073880668998)
XLA Ops:
  10.9 22.2 %all_to_all.19 = s32[64,1,2]{2,1,0:T(1,128)S(1)} all-to-all(s32[64,1,2]{2,1,0:T(1,128)S(1)} %bitcast.340), channel_id=1, replica_groups=mesh['seq'=64,'head'=4] {'seq'}, dimensions={0} | all-to-all | bytes 1024 | tf_op jit(solution)/shard_map/all_to_all | solution.py:167
  34.5 3.1 gather_fusion.3
  37.6 3.0 gather_fusion.2
  40.6 7.5 pad_maximum_fusion
  48.1 5.9 all-to-all-start.1
  55.2 184.7 %all-to-all-done.1 = bf16[64,2,2,128,128]{4,3,1,2,0:T(8,128)(2,1)} async-done(((bf16[64,2,2,128,128]{4,3,1,2,0:T(8,128)(2,1)}), bf16[64,2,2,128,128]{4,3,1,2,0:T(8,128)(2,1)}, u32[]{:S(2)}, u32[]{:S(2)}) %all-to-all-start.1) | async-done | bytes 8388640 | tf_op jit(solution)/shard_map/all_to_all | solution.py:172
  239.8 10.3 %copy.256 = bf16[64,2,2,128,128]{4,3,2,1,0:T(8,128)(2,1)} copy(bf16[64,2,2,128,128]{4,3,1,2,0:T(8,128)(2,1)} %all-to-all-done.1) | data formatting | bytes 16777216 | tf_op jit(solution)/shard_map/all_to_all | solution.py:172
  250.2 5.4 gather_fusion.4
  255.6 1.9 copy.257
  263.3 1.9 copy.289
  265.2 3.5 copy.290
  268.7 7.9 broadcast_in_dim.17
  276.6 7.7 scatter_fusion
  284.2 9.2 convert_element_type.120
  293.4 6.3 all-to-all-start.2
  300.5 3.5 collective-permute-start
  304.0 1.9 collective-permute-start.1
  307.2 409.5 %all-reduce.6 = bf16[2,2,128,128]{3,2,0,1:T(8,128)(2,1)S(1)} all-reduce(f32[2,2,128,128]{3,2,0,1:T(8,128)S(1)} %convert_multiply_fusion.1), channel_id=1, replica_groups=mesh['seq'=64,'head'=4] {'seq'}, use_global_device_ids=true, to_apply=%region_1.0 | all-reduce | flops 65536 | bytes 393216 | tf_op jit(solution)/shard_map/psum | solution.py:132
  730.7 2.1 convolution_bitcast_fusion.10
  735.9 1.3 convolution_bitcast_fusion.12
  737.9 1.7 pad_maximum_fusion.5
  748.2 3.6 collective-permute-start.2
  751.8 5.7 collective-permute-start.3
  760.4 1.5 fusion.80
  761.9 133.5 %all-reduce.5.cloned.1.call-done = f32[2,2,128,128]{2,3,1,0:T(8,128)} async-done(((f32[2,2,128,128]{2,3,1,0:T(8,128)}), f32[2,2,128,128]{2,3,1,0:T(8,128)}) %all-reduce.5.cloned.1.call-update) | async-done | bytes 262160 | tf_op jit(solution)/shard_map/psum | solution.py:149
  895.4 2.3 slice_multiply_fusion
  897.7 2.1 fusion.76
  899.8 2.1 fusion.77
  901.9 2.1 fusion.79
  906.6 13.3 %reshape_reshape.6 = bf16[128,32768]{1,0:T(8,128)(2,1)} reshape(bf16[64,2,2,128,128]{4,3,2,1,0:T(8,128)(2,1)} %all-to-all-done.2) | data formatting | bytes 16777216 | tf_op jit(solution)/shard_map/reshape;reshape | solution.py:53
  919.9 4.8 fusion.84
  925.6 1.6 convolution_add_fusion
  (191 shorter events, 46.7 us)
Async XLA Ops:
  7.2 27.3 %copy-start = (bf16[1024,128]{1,0:T(8,128)(2,1)S(1)}, bf16[1024,128]{1,0:T(8,128)(2,1)}, u32[]{:S(2)}) copy-start(bf16[1024,128]{1,0:T(8,128)(2,1)} %param.39) | copy-start | bytes 786436
  34.5 3.1 copy-start.1
  48.1 6.0 copy-start.26
  48.1 6.2 copy-start.27
  48.1 6.4 copy-start.25
  48.1 191.7 %all-to-all-start.1 = ((bf16[64,2,2,128,128]{4,3,1,2,0:T(8,128)(2,1)}), bf16[64,2,2,128,128]{4,3,1,2,0:T(8,128)(2,1)}, u32[]{:S(2)}, u32[]{:S(2)}) async-start(bf16[64,2,2,128,128]{4,3,1,2,0:T(8,128)(2,1)} %pad_maximum_fusion), calls=%async_computation.1 | async-start | bytes 16777216 | tf_op jit(solution)/shard_map/all_to_all | solution.py:172
  250.2 7.3 copy-start.24
  259.1 2.0 copy-start.7
  259.5 2.1 copy-start.9
  260.7 1.4 copy-start.11
  293.4 12.5 %copy-start.29 = (s32[2]{0:T(128)S(1)}, s32[2]{0:T(128)}, u32[]{:S(2)}) copy-start(s32[2]{0:T(128)} %param.45) | copy-start | bytes 28
  293.4 613.1 %all-to-all-start.2 = ((bf16[64,2,2,128,128]{4,3,2,1,0:T(8,128)(2,1)}), bf16[64,2,2,128,128]{4,3,2,1,0:T(8,128)(2,1)}, u32[]{:S(2)}, u32[]{:S(2)}) async-start(bf16[64,2,2,128,128]{4,3,2,1,0:T(8,128)(2,1)} %bitcast.283), calls=%async_computation.2 | async-start | bytes 16777216 | tf_op jit(solution)/shard_map/all_to_all | solution.py:198
  299.8 595.6 %all-reduce.5.cloned.1.call-start = ((), (), s32[]{:S(2)}) async-start(), calls=%async_computation.3 | async-start | bytes 524288 | tf_op jit(solution)/shard_map/psum | solution.py:149
  300.5 437.4 %collective-permute-start = (bf16[2,128,128]{2,1,0:T(8,128)(2,1)}, bf16[2,128,128]{2,1,0:T(8,128)(2,1)}, u32[]{:S(2)}, u32[]{:S(2)}) collective-permute-start(bf16[2,128,128]{2,1,0:T(8,128)(2,1)} %get-tuple-element.192), channel_id=1, source_target_pairs={{0,4},{4,8},{8,12},{12,16},{16,20},{20,24},{24,28},{28,32},{32,36}... | collective-permute-start | bytes 196616 | tf_op jit(solution)/shard_map/ppermute | solution.py:17
  304.0 433.8 %collective-permute-start.1 = (bf16[2,128,128]{2,1,0:T(8,128)(2,1)}, bf16[2,128,128]{2,1,0:T(8,128)(2,1)}, u32[]{:S(2)}, u32[]{:S(2)}) collective-permute-start(bf16[2,128,128]{2,1,0:T(8,128)(2,1)} %get-tuple-element.193), channel_id=1, source_target_pairs={{4,0},{8,4},{12,8},{16,12},{20,16},{24,20},{28,24},{32,28},{36,32}... | collective-permute-start | bytes 196616 | tf_op jit(solution)/shard_map/ppermute | solution.py:18
  719.5 9.4 copy-start.28
  728.9 5.6 copy-start.21
  739.6 3.3 copy-start.23
  744.9 1.2 copy-start.4
  745.8 1.2 copy-start.6
  746.2 1.1 copy-start.20
  748.2 11.3 %collective-permute-start.2 = (bf16[2,128,128]{1,2,0:T(8,128)(2,1)S(1)}, bf16[2,128,128]{1,2,0:T(8,128)(2,1)S(1)}, u32[]{:S(2)}, u32[]{:S(2)}) collective-permute-start(bf16[2,128,128]{1,2,0:T(8,128)(2,1)S(1)} %get-tuple-element.201), channel_id=1, source_target_pairs={{0,4},{4,8},{8,12},{12,16},{16,20},{20,24},{24,28},{28,32},{32,36}... | collective-permute-start | bytes 196616 | tf_op jit(solution)/shard_map/ppermute | solution.py:17
  751.8 152.2 %copy-start.8 = (bf16[8,2,128,128]{3,2,1,0:T(8,128)(2,1)S(1)}, bf16[8,2,128,128]{3,2,1,0:T(8,128)(2,1)}, u32[]{:S(2)}) copy-start(bf16[8,2,128,128]{3,2,1,0:T(8,128)(2,1)} %copy-done.7) | copy-start | bytes 1572868
  751.8 7.7 collective-permute-start.3
  758.6 145.7 %copy-start.10 = (bf16[8,2,128,128]{3,2,1,0:T(8,128)(2,1)S(1)}, bf16[8,2,128,128]{3,2,1,0:T(8,128)(2,1)}, u32[]{:S(2)}) copy-start(bf16[8,2,128,128]{3,2,1,0:T(8,128)(2,1)} %copy-done.9) | copy-start | bytes 1572868
  895.4 9.2 copy-start.12
  895.4 9.5 %copy-start.15 = (f32[8,128,2,64]{1,3,2,0:T(8,128)S(1)}, f32[8,128,2,64]{1,3,2,0:T(8,128)}, u32[]{:S(2)}) copy-start(f32[8,128,2,64]{1,3,2,0:T(8,128)} %convolution_bitcast_fusion.9) | copy-start | bytes 1572868
  895.4 9.5 %copy-start.16 = (f32[8,128,2,64]{1,3,2,0:T(8,128)S(1)}, f32[8,128,2,64]{1,3,2,0:T(8,128)}, u32[]{:S(2)}) copy-start(f32[8,128,2,64]{1,3,2,0:T(8,128)} %convolution_bitcast_fusion.10) | copy-start | bytes 1572868
  895.4 9.5 %copy-start.17 = (f32[8,128,2,64]{1,3,2,0:T(8,128)S(1)}, f32[8,128,2,64]{1,3,2,0:T(8,128)}, u32[]{:S(2)}) copy-start(f32[8,128,2,64]{1,3,2,0:T(8,128)} %convolution_bitcast_fusion.12) | copy-start | bytes 1572868
  895.4 9.5 %copy-start.18 = (f32[8,128,2,64]{1,3,2,0:T(8,128)S(1)}, f32[8,128,2,64]{1,3,2,0:T(8,128)}, u32[]{:S(2)}) copy-start(f32[8,128,2,64]{1,3,2,0:T(8,128)} %convolution_bitcast_fusion.11) | copy-start | bytes 1572868
  919.9 5.8 copy-start.2
  927.2 3.0 copy-start.14
  (5 other events, 4.6 us)
Sparse Core Ops, SparseCore 0:
  721.2 174.0 all-reduce.4
where the time goes:
time: 940 us; the launch traced here: 939 us
  blocking collectives  432 us (46%)
  waiting for transfers between devices  318 us (34%)
  local copies, waits for them, and re-layouts  81.8 us (9%)
  other arithmetic  35.3 us (4%)
  starting transfers between devices  27 us (3%)
  matrix products  25.8 us (3%)
  between operations  18.7 us (2%)
    psum x1, blocking collectives, shards(): shared = lax.psum(own_part, 'seq').astype(jnp.bfloat16)  409 us
    all_to_all x1, waiting for transfers between devices, shards(): lax.all_to_all(outgoing.reshape(owners, capacity, 2, BLOCK, features), 's...  185 us
    psum x1, waiting for transfers between devices, shards(): totals = lax.psum(jnp.stack(global_pieces), 'seq')  133 us
    all_to_all x1, blocking collectives, shards(): lax.all_to_all(requested.reshape(owners, capacity), 'seq', split_axis=0,...  22.2 us
  transfers between devices with their start and end apart: 7, of which 2 were waited for; matrix products, arithmetic and copies ran while one was open for 5% of the time, Pallas kernels for 0%

commit v1 on v0

--- a/solution.py
+++ b/solution.py
@@ -3,6 +3,7 @@
 import jax.numpy as jnp
 from jax import lax
 from jax.sharding import PartitionSpec as P
+from jax.lax import all_gather
 
 BLOCK = 128
 
@@ -146,7 +147,8 @@
                 ]
             )
         )
-    totals = lax.psum(jnp.stack(global_pieces), "seq")
+    guide_the_signs = lambda xs: jnp.sum(all_gather(xs, "seq"), axis=0)
+    totals = guide_the_signs(jnp.stack(global_pieces))
     for number in range(shared.shape[0]):
         d_keys = d_keys.at[global_local[number]].add(
             owned_here[number] * totals[number, 0].reshape(block_shape[1:])

time: 940 us -> 853 us (0.907)
  blocking collectives: 432 us -> 246 us
  waiting for transfers between devices: 318 us -> 393 us
  starting transfers between devices: 27 us -> 41 us
  local copies, waits for them, and re-layouts: 81.8 us -> 92.7 us
    psum x1, blocking collectives: 409 us -> 246 us  [shards(): shared = lax.psum(own_part, 'seq').astype(jnp.bfloat16)]
    ppermute x2, waiting for transfers between devices: 0.01 us -> 156 us  [extended(): before = lax.ppermute(last, axis, up)]
    psum x1 -> x0, waiting for transfers between devices: 133 us -> none  [shards(): totals = lax.psum(jnp.stack(global_pieces), 'seq')]
    all_to_all x1, waiting for transfers between devices: 185 us -> 231 us  [shards(): lax.all_to_all(outgoing.reshape(owners, capacity, 2, BLOCK, features), 's...]
    all_to_all x1 -> x0, blocking collectives: 22.2 us -> none  [shards(): lax.all_to_all(requested.reshape(owners, capacity), 'seq', split_axis=0,...]
    all_to_all x0 -> x1, starting transfers between devices: none -> 13.2 us  [shards(): lax.all_to_all(requested.reshape(owners, capacity), 'seq', split_axis=0,...]
  transfers between devices with their start and end apart: 7 -> 8, of which waited for: 2 -> 4; matrix products, arithmetic and copies ran while one was open for 5% -> 13% of each run, Pallas kernels for 0% -> 0%
where the time goes in v1:
time: 853 us; the launch traced here: 851 us
  waiting for transfers between devices  393 us (46%)
  blocking collectives  246 us (29%)
  local copies, waits for them, and re-layouts  92.7 us (11%)
  starting transfers between devices  41 us (5%)
  other arithmetic  33.8 us (4%)
  matrix products  25.9 us (3%)
  between operations  19 us (2%)
    psum x1, blocking collectives, shards(): shared = lax.psum(own_part, 'seq').astype(jnp.bfloat16)  246 us
    all_to_all x1, waiting for transfers between devices, shards(): lax.all_to_all(outgoing.reshape(owners, capacity, 2, BLOCK, features), 's...  231 us
    ppermute x2, waiting for transfers between devices, extended(): before = lax.ppermute(last, axis, up)  156 us
  transfers between devices with their start and end apart: 8, of which 4 were waited for; matrix products, arithmetic and copies ran while one was open for 13% of the time, Pallas kernels for 0%

profile of v1, /device:TPU:1, one launch (start us, length us, event | category | flops | bytes accessed | tf_op | source)
XLA Modules:
  0.0 851.3 jit_solution(18232944805550063768)
XLA Ops:
  11.5 13.2 %all-to-all-start = ((s32[64,1,2]{2,1,0:T(1,128)}), s32[64,1,2]{2,1,0:T(1,128)S(1)}, u32[]{:S(2)}, u32[]{:S(2)}) async-start(s32[64,1,2]{2,1,0:T(1,128)} %bitcast.23), calls=%async_computation | async-start | bytes 65536 | tf_op jit(solution)/shard_map/all_to_all | solution.py:169
  29.1 245.9 %all-reduce.3 = bf16[2,2,128,128]{3,2,0,1:T(8,128)(2,1)S(1)} all-reduce(f32[2,2,128,128]{3,2,0,1:T(8,128)S(1)} %convert_multiply_fusion.1), channel_id=1, replica_groups=mesh['seq'=64,'head'=4] {'seq'}, use_global_device_ids=true, to_apply=%region_1.0 | all-reduce | flops 65536 | bytes 393216 | tf_op jit(solution)/shard_map/psum | solution.py:133
  280.9 3.0 gather_fusion.3
  284.0 3.0 gather_fusion.2
  287.0 7.5 pad_maximum_fusion
  294.5 10.9 %all-to-all-start.1 = ((bf16[64,2,2,128,128]{4,3,1,2,0:T(8,128)(2,1)}), bf16[64,2,2,128,128]{4,3,1,2,0:T(8,128)(2,1)}, u32[]{:S(2)}, u32[]{:S(2)}) async-start(bf16[64,2,2,128,128]{4,3,1,2,0:T(8,128)(2,1)} %pad_maximum_fusion), calls=%async_computation.1 | async-start | bytes 16777216 | tf_op jit(solution)/shard_map/all_to_all | solution.py:174
  309.6 230.8 %all-to-all-done.1 = bf16[64,2,2,128,128]{4,3,1,2,0:T(8,128)(2,1)} async-done(((bf16[64,2,2,128,128]{4,3,1,2,0:T(8,128)(2,1)}), bf16[64,2,2,128,128]{4,3,1,2,0:T(8,128)(2,1)}, u32[]{:S(2)}, u32[]{:S(2)}) %all-to-all-start.1) | async-done | bytes 8388640 | tf_op jit(solution)/shard_map/all_to_all | solution.py:174
  540.3 10.3 %copy.427 = bf16[64,2,2,128,128]{4,3,2,1,0:T(8,128)(2,1)} copy(bf16[64,2,2,128,128]{4,3,1,2,0:T(8,128)(2,1)} %all-to-all-done.1) | data formatting | bytes 16777216 | tf_op jit(solution)/shard_map/all_to_all | solution.py:174
  550.7 5.4 gather_fusion.4
  556.1 1.9 copy.428
  564.5 1.9 copy.463
  566.4 3.5 copy.464
  569.9 7.9 broadcast_in_dim.17
  577.8 7.7 scatter_fusion
  585.5 9.2 %convert_element_type.120 = bf16[128,2,128,128]{3,2,1,0:T(8,128)(2,1)} convert(f32[128,2,128,128]{3,2,1,0:T(8,128)} %scatter_fusion) | non-fusion elementwise | flops 4194304 | bytes 25165824 | tf_op jit(solution)/shard_map/convert_element_type | solution.py:201
  594.7 6.2 all-to-all-start.2
  601.6 3.5 collective-permute-start
  605.1 2.1 collective-permute-start.1
  617.1 2.1 convolution_bitcast_fusion.10
  620.8 1.6 fusion.25
  624.5 156.2 %collective-permute-done = bf16[2,128,128]{2,1,0:T(8,128)(2,1)} collective-permute-done((bf16[2,128,128]{2,1,0:T(8,128)(2,1)}, bf16[2,128,128]{2,1,0:T(8,128)(2,1)}, u32[]{:S(2)}, u32[]{:S(2)}) %collective-permute-start) | collective-permute-done | bytes 65568 | tf_op jit(solution)/shard_map/ppermute | solution.py:18
  780.7 3.4 collective-permute-done.1
  784.1 1.7 pad_maximum_fusion.5
  785.8 2.0 reshape.742
  787.8 2.0 reshape.748
  791.1 2.0 reshape.751
  799.7 2.1 collective-permute-start.2
  801.8 2.8 collective-permute-start.3
  804.9 2.5 collective-permute-done.3
  810.1 6.6 reduce_sum.72
  820.3 13.4 %reshape_reshape.6 = bf16[128,32768]{1,0:T(8,128)(2,1)} reshape(bf16[64,2,2,128,128]{4,3,2,1,0:T(8,128)(2,1)} %all-to-all-done.2) | data formatting | bytes 16777216 | tf_op jit(solution)/shard_map/reshape;reshape | solution.py:54
  833.7 4.8 fusion.84
  (176 shorter events, 55.1 us)
Async XLA Ops:
  7.2 273.7 %copy-start = (bf16[1024,128]{1,0:T(8,128)(2,1)S(1)}, bf16[1024,128]{1,0:T(8,128)(2,1)}, u32[]{:S(2)}) copy-start(bf16[1024,128]{1,0:T(8,128)(2,1)} %param.39) | copy-start | bytes 786436
  11.5 268.0 %all-to-all-start = ((s32[64,1,2]{2,1,0:T(1,128)}), s32[64,1,2]{2,1,0:T(1,128)S(1)}, u32[]{:S(2)}, u32[]{:S(2)}) async-start(s32[64,1,2]{2,1,0:T(1,128)} %bitcast.23), calls=%async_computation | async-start | bytes 65536 | tf_op jit(solution)/shard_map/all_to_all | solution.py:169
  280.9 3.1 copy-start.1
  294.5 11.1 %copy-start.17 = (f32[2,1024]{1,0:T(2,128)S(1)}, f32[2,1024]{1,0:T(2,128)}, u32[]{:S(2)}) copy-start(f32[2,1024]{1,0:T(2,128)} %param.42) | copy-start | bytes 24580
  294.5 245.9 %all-to-all-start.1 = ((bf16[64,2,2,128,128]{4,3,1,2,0:T(8,128)(2,1)}), bf16[64,2,2,128,128]{4,3,1,2,0:T(8,128)(2,1)}, u32[]{:S(2)}, u32[]{:S(2)}) async-start(bf16[64,2,2,128,128]{4,3,1,2,0:T(8,128)(2,1)} %pad_maximum_fusion), calls=%async_computation.1 | async-start | bytes 16777216 | tf_op jit(solution)/shard_map/all_to_all | solution.py:174
  305.4 504.8 %all-gather.3.cloned.1.call-start = ((), (), s32[]{:S(2)}) async-start(), calls=%async_computation.3 | async-start | bytes 17039360 | tf_op jit(solution)/shard_map/all_gather | solution.py:150
  307.9 242.8 %copy-start.14 = (bf16[8,2,128,128]{3,2,1,0:T(8,128)(2,1)}, bf16[8,2,128,128]{3,2,1,0:T(8,128)(2,1)S(1)}, u32[]{:S(2)}) copy-start(bf16[8,2,128,128]{3,2,1,0:T(8,128)(2,1)S(1)} %fusion.27) | copy-start | bytes 1572868
  558.7 1.8 copy-start.5
  560.5 0.8 copy-start.7
  562.5 0.9 copy-start.9
  594.7 20.6 %copy-start.18 = (s32[4]{0:T(128)S(1)}, s32[4]{0:T(128)}, u32[]{:S(2)}) copy-start(s32[4]{0:T(128)} %constant.366.clone.1) | copy-start | bytes 52
  594.7 225.7 %all-to-all-start.2 = ((bf16[64,2,2,128,128]{4,3,2,1,0:T(8,128)(2,1)}), bf16[64,2,2,128,128]{4,3,2,1,0:T(8,128)(2,1)}, u32[]{:S(2)}, u32[]{:S(2)}) async-start(bf16[64,2,2,128,128]{4,3,2,1,0:T(8,128)(2,1)} %bitcast.284), calls=%async_computation.2 | async-start | bytes 16777216 | tf_op jit(solution)/shard_map/all_to_all | solution.py:200
  601.6 179.1 %collective-permute-start = (bf16[2,128,128]{2,1,0:T(8,128)(2,1)}, bf16[2,128,128]{2,1,0:T(8,128)(2,1)}, u32[]{:S(2)}, u32[]{:S(2)}) collective-permute-start(bf16[2,128,128]{2,1,0:T(8,128)(2,1)} %get-tuple-element.198), channel_id=1, source_target_pairs={{0,4},{4,8},{8,12},{12,16},{16,20},{20,24},{24,28},{28,32},{32,36}... | collective-permute-start | bytes 196616 | tf_op jit(solution)/shard_map/ppermute | solution.py:18
  605.1 179.0 %collective-permute-start.1 = (bf16[2,128,128]{2,1,0:T(8,128)(2,1)}, bf16[2,128,128]{2,1,0:T(8,128)(2,1)}, u32[]{:S(2)}, u32[]{:S(2)}) collective-permute-start(bf16[2,128,128]{2,1,0:T(8,128)(2,1)} %get-tuple-element.199), channel_id=1, source_target_pairs={{4,0},{8,4},{12,8},{16,12},{20,16},{24,20},{28,24},{32,28},{36,32}... | collective-permute-start | bytes 196616 | tf_op jit(solution)/shard_map/ppermute | solution.py:19
  619.7 1.1 copy-start.3
  795.4 1.0 copy-start.16
  796.2 1.4 copy-start.4
  797.2 1.4 copy-start.15
  799.4 8.1 copy-start.6
  799.5 8.4 copy-start.8
  799.6 8.6 %copy-start.10 = (bf16[8,2,128,128]{3,2,1,0:T(8,128)(2,1)S(1)}, bf16[8,2,128,128]{3,2,1,0:T(8,128)(2,1)}, u32[]{:S(2)}) copy-start(bf16[8,2,128,128]{3,2,1,0:T(8,128)(2,1)} %copy-done.9) | copy-start | bytes 1572868
  799.7 5.3 collective-permute-start.2
  801.7 6.7 copy-start.11
  801.7 6.7 copy-start.12
  801.7 6.7 copy-start.13
  801.8 5.7 collective-permute-start.3
  833.7 5.8 copy-start.2
Sparse Core Ops, SparseCore 0:
  309.7 216.6 all-gather.2
